TPU v7x, 256 devices: a whole 4x4x8 slice. The times are simulated.
256 devices in a mesh: grp: 8 (over z), ord: 32 (over x, y, core).
Axes of the slice: x: 4, y: 4, z: 8, core: 2. Of those that a mesh axis runs over, the one named last changes fastest.
Arguments:
- legendre: float32 [512, 1048576], P('ord', 'grp')
- lon_center: float32 [8], P('grp'), may hold values from 0 to 1
- counts: int32 [8, 32], P('grp'), may hold values from 1 to 4096, 98304 in all within a row
- column_index: int32 [3, 512], replicated, may hold values from 0 to 120, as said below
Outputs:
- factor: float32 [512, 512], replicated
Inputs may be any that keep to these rules, and one draw needn't show every extreme that they name: `column_index`: each column names a different coefficient: row 0 is its degree (at most 120), row 1 its order (at most the degree), row 2 is 1 for a sine term and 0 for a cosine term, and 0 at order 0. Each group's counts add up to 98304.
All inputs are finite; a program needn't handle non-finite values.
Results may differ from a plain program's by a relative error of at most 0.0003.
Values sent between devices are 32-bit elements; how exact they have to be, the bound alone decides.
A program may use at most 64 MiB of HBM per device.

v0:
```python
import math
import jax
import jax.numpy as jnp
from jax import lax
from jax.sharding import PartitionSpec as P

NMAX = 120
quarter_turn = math.pi / 2
track_span = 0.3
kaula_gain = 1.2
highest = lax.Precision.HIGHEST


def upper_factor(matrix):
    return jnp.linalg.cholesky(matrix).T


def block_grams(exchanged):
    blocks = exchanged[:, 0]
    return jnp.einsum("jkb,lkb->kjl", blocks, blocks, precision=highest)


def body(legendre, lon_center, counts, column_index):
    ord_size = lax.axis_size("ord")
    grp_size = lax.axis_size("grp")
    cols_dev, rows_grp = legendre.shape
    rows_dev = rows_grp // ord_size
    scaling = 1.0 / math.sqrt(rows_grp * grp_size)
    own_columns = lax.dynamic_slice_in_dim(
        column_index, lax.axis_index("ord") * cols_dev, cols_dev, 1
    )
    harmonic = own_columns[1].astype(jnp.float32)
    sine_part = own_columns[2].astype(jnp.float32)
    longitude = lon_center[0] + jnp.arange(rows_grp, dtype=jnp.float32) * (track_span / rows_grp)
    harmonic_wave = jnp.cos(
        harmonic[:, None] * longitude[None, :] - sine_part[:, None] * quarter_turn
    )
    slot_index = jnp.arange(rows_dev, dtype=jnp.int32)
    row_valid = (slot_index[None, :] < counts[0][:, None]).astype(jnp.float32).reshape(rows_grp)
    design = legendre * harmonic_wave * (row_valid * scaling)[None, :]
    block_rows = min(512, rows_dev)
    shaped = design.reshape(cols_dev, ord_size, rows_dev // block_rows, block_rows)
    block_gram = block_grams(lax.all_to_all(shaped, "ord", split_axis=1, concat_axis=0, tiled=True))
    local_gram = jnp.sum(block_gram, axis=0)
    degree = column_index[0].astype(jnp.float32)
    kaula_weight = kaula_gain * (degree / NMAX) ** 2
    regular = jnp.diag(kaula_weight * kaula_weight)
    normal = lax.psum(local_gram, ("grp", "ord")) + regular
    return upper_factor(normal)


def solution(mesh):
    placed = (P("ord", "grp"), P("grp"), P("grp", None), P())
    return jax.shard_map(body, mesh=mesh, in_specs=placed, out_specs=P(), check_vma=False)
```

profile of v0, /device:TPU:2, one launch (start us, length us, event | category | flops | bytes accessed | tf_op | source)
XLA Modules:
  0.0 538.6 jit_solution(2535784197587066006)
XLA Ops:
  6.5 0.0 all-reduce.3.cloned.1.call-start
  6.5 0.8 constant_dynamic-slice_fusion
  7.3 0.8 select_bitcast_fusion.1
  8.1 0.1 copy.40
  8.8 0.2 multiply_add_fusion
  9.0 29.6 %multiply_multiply_fusion = f32[16,131072]{1,0:T(8,128)S(1)} fusion(f32[16,131072]{1,0:T(8,128)} %param.4, f32[131072]{0:T(1024)S(1)} %bitcast.48, f32[16]{0:T(128)S(1)} %multiply_bitcast_fusion, f32[131072]{0:T(1024)S(1)} %multiply_add_fusion, f32[16]{0:T(128)S(1)} %convert_bitcast_fusion), kind=kLoop, calls=%fused_computation | loop fusion | flops 8388608 | bytes 17825920 | tf_op jit(solution)/shard_map/mul | solution.py:40
  38.6 4.9 copy.41
  43.5 20.4 %copy.25 = f32[16,32,8,512]{3,0,2,1:T(8,128)S(1)} copy(f32[16,32,8,512]{3,2,1,0:T(8,128)S(1)} %bitcast.46) | data formatting | bytes 16777216 | tf_op jit(solution)/shard_map/reshape | solution.py:42
  63.8 100.5 %all_to_all.15 = f32[16,32,8,512]{3,0,2,1:T(8,128)S(1)} all-to-all(f32[16,32,8,512]{3,0,2,1:T(8,128)S(1)} %copy.25), channel_id=1, replica_groups=mesh['grp'=8,'ord'=32] {'ord'}, dimensions={1} | all-to-all | bytes 16777216 | tf_op jit(solution)/shard_map/all_to_all | solution.py:43
  164.3 1.9 copy.26
  166.2 16.1 %convolution_bitcast_fusion = f32[512,512]{0,1:T(8,128)} fusion(f32[512,8,512]{2,0,1:T(8,128)S(1)} %bitcast.44), kind=kOutput, calls=%fused_computation.1 | convolution fusion | flops 12884901888 | bytes 9437184 | tf_op jit(solution)/shard_map/jkb,lkb->kjl/dot_general | solution.py:20
  182.4 0.0 all-reduce.3.cloned.1.call-update
  182.4 0.7 multiply_multiply_fusion.1
  183.1 259.9 %all-reduce.3.cloned.1.call-done = f32[512,512]{0,1:T(8,128)} async-done(((f32[512,512]{0,1:T(8,128)}), f32[512,512]{0,1:T(8,128)}) %all-reduce.3.cloned.1.call-update) | async-done | bytes 1048592 | tf_op jit(solution)/shard_map/psum | solution.py:48
  443.0 1.3 select_add_fusion
  444.3 0.3 copy.28
  444.7 1.4 fusion
  446.1 11.7 %cholesky.103 = f32[128,128]{1,0:T(8,128)S(1)} custom-call(f32[128,128]{1,0:T(8,128)S(1)} %cholesky.263), custom_call_target="Cholesky" | custom-call | tf_op jit(solution)/shard_map/jit(cholesky)/cholesky | solution.py:15
  457.9 9.8 %custom-call.27 = f32[1,128,128]{1,2,0:T(8,128)S(1)} custom-call(f32[1,128,128]{2,1,0:T(8,128)S(1)} %get-tuple-element.10), custom_call_target="InvertDiagBlocksLowerTriangular" | custom-call | tf_op jit(solution)/shard_map/jit(cholesky)/cholesky | solution.py:15
  467.7 0.3 fusion.3
  468.0 0.3 convolution_subtract_fusion
  468.4 11.7 %cholesky.215 = f32[128,128]{1,0:T(8,128)S(1)} custom-call(f32[128,128]{1,0:T(8,128)S(1)} %cholesky.267), custom_call_target="Cholesky" | custom-call | tf_op jit(solution)/shard_map/jit(cholesky)/cholesky | solution.py:15
  480.1 0.1 copy.31
  480.2 0.1 copy.30
  480.3 0.1 copy.29
  480.5 9.9 %custom-call.28 = f32[1,128,128]{1,2,0:T(8,128)S(1)} custom-call(f32[1,128,128]{2,1,0:T(8,128)S(1)} %get-tuple-element.8), custom_call_target="InvertDiagBlocksLowerTriangular" | custom-call | tf_op jit(solution)/shard_map/jit(cholesky)/cholesky | solution.py:15
  490.4 0.1 cholesky.222
  490.6 0.3 convolution_dynamic-update-slice_fusion
  490.9 0.6 convolution_subtract_fusion.1
  491.5 11.7 %cholesky.236 = f32[128,128]{1,0:T(8,128)S(1)} custom-call(f32[128,128]{1,0:T(8,128)S(1)} %cholesky.272), custom_call_target="Cholesky" | custom-call | tf_op jit(solution)/shard_map/jit(cholesky)/cholesky | solution.py:15
  503.3 0.1 copy.33
  503.4 9.8 %custom-call.29 = f32[1,128,128]{1,2,0:T(8,128)S(1)} custom-call(f32[1,128,128]{2,1,0:T(8,128)S(1)} %get-tuple-element.6), custom_call_target="InvertDiagBlocksLowerTriangular" | custom-call | tf_op jit(solution)/shard_map/jit(cholesky)/cholesky | solution.py:15
  513.2 0.3 convolution_dynamic-update-slice_fusion.1
  513.5 0.5 convolution_subtract_fusion.2
  514.0 11.7 %cholesky.253 = f32[128,128]{1,0:T(8,128)S(1)} custom-call(f32[128,128]{1,0:T(8,128)S(1)} %convolution_subtract_fusion.2), custom_call_target="Cholesky" | custom-call | tf_op jit(solution)/shard_map/jit(cholesky)/cholesky | solution.py:15
  525.7 0.1 copy.35
  525.8 0.7 compare_reduce_fusion.1
  526.5 0.6 compare_reduce_fusion
  527.2 0.7 compare_reduce_fusion.2
  530.4 1.1 select_bitcast_fusion
  (13 shorter events, 0.2 us)
Async XLA Ops:
  6.5 436.4 %all-reduce.3.cloned.1.call-start = ((), (), s32[]{:S(2)}) async-start(), calls=%async_computation.1 | async-start | bytes 2097152 | tf_op jit(solution)/shard_map/psum | solution.py:48
Sparse Core Ops, SparseCore 0:
  182.5 260.4 all-reduce.2
where the time goes:
time: 542 us; the launch traced here: 539 us
  waiting for transfers between devices  260 us (48%)
  other arithmetic  114 us (21%)
  blocking collectives  100 us (18%)
  local copies, waits for them, and re-layouts  29 us (5%)
  matrix products  18.5 us (3%)
  between operations  17 us (3%)
    psum x1, waiting for transfers between devices, body(): normal = lax.psum(local_gram, ('grp', 'ord')) + regular  260 us
    all_to_all x1, blocking collectives, body(): lax.all_to_all(shaped, 'ord', split_axis=1, concat_axis=0, tiled=True)  100 us
    another operation x14, other arithmetic, upper_factor(): return jnp.linalg.cholesky(matrix).T  78.6 us
    mul x1, other arithmetic, body(): design = legendre * harmonic_wave * (row_valid * scaling)[None, :]  29.6 us
    reshape x1, local copies, waits for them, and re-layouts, body(): design.reshape(cols_dev, ord_size, rows_dev // block_rows, block_rows)  20.4 us
    dot_general x1, matrix products, block_grams(): return jnp.einsum('jkb,lkb->kjl', blocks, blocks, precision=highest)  16.1 us
  transfers between devices with their start and end apart: 1, of which 1 were waited for; matrix products, arithmetic and copies ran while one was open for 0% of the time, Pallas kernels for 0%

commit v1 on v0

--- a/solution.py
+++ b/solution.py
@@ -45,7 +45,7 @@
     degree = column_index[0].astype(jnp.float32)
     kaula_weight = kaula_gain * (degree / NMAX) ** 2
     regular = jnp.diag(kaula_weight * kaula_weight)
-    normal = lax.psum(local_gram, ("grp", "ord")) + regular
+    normal = lax.psum(lax.psum(local_gram, "grp"), "ord") + regular
     return upper_factor(normal)
 
 

time: 542 us -> 477 us (0.88)
  waiting for transfers between devices: 260 us -> 194 us
    psum x1 -> x2, waiting for transfers between devices: 260 us -> 194 us  [body(): normal = lax.psum(lax.psum(local_gram, 'grp'), 'ord') + regular]
  transfers between devices with their start and end apart: 1 -> 2, of which waited for: 1 -> 2; matrix products, arithmetic and copies ran while one was open for 0% -> 0% of each run, Pallas kernels for 0% -> 0%
where the time goes in v1:
time: 477 us; the launch traced here: 472 us
  waiting for transfers between devices  194 us (41%)
  other arithmetic  114 us (24%)
  blocking collectives  100 us (21%)
  local copies, waits for them, and re-layouts  29 us (6%)
  matrix products  18.4 us (4%)
  between operations  17 us (4%)
    psum x2, waiting for transfers between devices, body(): normal = lax.psum(lax.psum(local_gram, 'grp'), 'ord') + regular  194 us
    all_to_all x1, blocking collectives, body(): lax.all_to_all(shaped, 'ord', split_axis=1, concat_axis=0, tiled=True)  100 us
    another operation x14, other arithmetic, upper_factor(): return jnp.linalg.cholesky(matrix).T  78.6 us
    mul x1, other arithmetic, body(): design = legendre * harmonic_wave * (row_valid * scaling)[None, :]  29.6 us
    reshape x1, local copies, waits for them, and re-layouts, body(): design.reshape(cols_dev, ord_size, rows_dev // block_rows, block_rows)  20.4 us
    dot_general x1, matrix products, block_grams(): return jnp.einsum('jkb,lkb->kjl', blocks, blocks, precision=highest)  16.1 us
  transfers between devices with their start and end apart: 2, of which 2 were waited for; matrix products, arithmetic and copies ran while one was open for 0% of the time, Pallas kernels for 0%

profile of v1, /device:TPU:2, one launch (start us, length us, event | category | flops | bytes accessed | tf_op | source)
XLA Modules:
  0.0 472.3 jit_solution(758496039798460978)
XLA Ops:
  6.5 0.0 all-reduce.4.cloned.1.call-start
  6.5 0.8 constant_dynamic-slice_fusion
  7.3 0.8 select_bitcast_fusion.1
  8.1 0.1 copy.40
  8.8 0.2 multiply_add_fusion
  9.0 29.6 %multiply_multiply_fusion = f32[16,131072]{1,0:T(8,128)S(1)} fusion(f32[16,131072]{1,0:T(8,128)} %param.4, f32[131072]{0:T(1024)S(1)} %bitcast.48, f32[16]{0:T(128)S(1)} %multiply_bitcast_fusion, f32[131072]{0:T(1024)S(1)} %multiply_add_fusion, f32[16]{0:T(128)S(1)} %convert_bitcast_fusion), kind=kLoop, calls=%fused_computation | loop fusion | flops 8388608 | bytes 17825920 | tf_op jit(solution)/shard_map/mul | solution.py:40
  38.6 4.9 %copy.41 = f32[2,8,256,512]{3,2,1,0:T(8,128)S(1)} copy(f32[2,8,256,512]{3,1,2,0:T(8,128)S(1)} %bitcast.45) | data formatting | bytes 16777216
  43.5 20.4 %copy.25 = f32[16,32,8,512]{3,0,2,1:T(8,128)S(1)} copy(f32[16,32,8,512]{3,2,1,0:T(8,128)S(1)} %bitcast.46) | data formatting | bytes 16777216 | tf_op jit(solution)/shard_map/reshape | solution.py:42
  63.9 100.5 %all_to_all.15 = f32[16,32,8,512]{3,0,2,1:T(8,128)S(1)} all-to-all(f32[16,32,8,512]{3,0,2,1:T(8,128)S(1)} %copy.25), channel_id=1, replica_groups=mesh['grp'=8,'ord'=32] {'ord'}, dimensions={1} | all-to-all | bytes 16777216 | tf_op jit(solution)/shard_map/all_to_all | solution.py:43
  164.3 1.9 copy.26
  166.3 16.1 %convolution_bitcast_fusion = f32[512,512]{0,1:T(8,128)} fusion(f32[512,8,512]{2,0,1:T(8,128)S(1)} %bitcast.44), kind=kOutput, calls=%fused_computation.1 | convolution fusion | flops 12884901888 | bytes 9437184 | tf_op jit(solution)/shard_map/jkb,lkb->kjl/dot_general | solution.py:20
  182.4 0.0 all-reduce.4.cloned.1.call-update
  182.4 0.0 all-reduce.6.cloned.1.call-start
  182.5 77.8 %all-reduce.4.cloned.1.call-done = f32[512,512]{0,1:T(8,128)} async-done(((f32[512,512]{0,1:T(8,128)}), f32[512,512]{0,1:T(8,128)}) %all-reduce.4.cloned.1.call-update) | async-done | bytes 1048592 | tf_op jit(solution)/shard_map/psum | solution.py:48
  260.3 0.0 all-reduce.6.cloned.1.call-update
  260.3 0.7 multiply_multiply_fusion.1
  261.0 115.7 %all-reduce.6.cloned.1.call-done = f32[512,512]{0,1:T(8,128)} async-done(((f32[512,512]{0,1:T(8,128)}), f32[512,512]{0,1:T(8,128)}) %all-reduce.6.cloned.1.call-update) | async-done | bytes 1048592 | tf_op jit(solution)/shard_map/psum | solution.py:48
  376.8 1.3 select_add_fusion
  378.1 0.3 copy.28
  378.4 1.4 fusion
  379.9 11.7 %cholesky.103 = f32[128,128]{1,0:T(8,128)S(1)} custom-call(f32[128,128]{1,0:T(8,128)S(1)} %cholesky.263), custom_call_target="Cholesky" | custom-call | tf_op jit(solution)/shard_map/jit(cholesky)/cholesky | solution.py:15
  391.7 9.8 %custom-call.27 = f32[1,128,128]{1,2,0:T(8,128)S(1)} custom-call(f32[1,128,128]{2,1,0:T(8,128)S(1)} %get-tuple-element.10), custom_call_target="InvertDiagBlocksLowerTriangular" | custom-call | tf_op jit(solution)/shard_map/jit(cholesky)/cholesky | solution.py:15
  401.5 0.3 fusion.3
  401.8 0.3 convolution_subtract_fusion
  402.1 11.7 %cholesky.215 = f32[128,128]{1,0:T(8,128)S(1)} custom-call(f32[128,128]{1,0:T(8,128)S(1)} %cholesky.267), custom_call_target="Cholesky" | custom-call | tf_op jit(solution)/shard_map/jit(cholesky)/cholesky | solution.py:15
  413.9 0.1 copy.31
  414.0 0.1 copy.30
  414.1 0.1 copy.29
  414.2 10.0 %custom-call.28 = f32[1,128,128]{1,2,0:T(8,128)S(1)} custom-call(f32[1,128,128]{2,1,0:T(8,128)S(1)} %get-tuple-element.8), custom_call_target="InvertDiagBlocksLowerTriangular" | custom-call | tf_op jit(solution)/shard_map/jit(cholesky)/cholesky | solution.py:15
  424.2 0.1 cholesky.222
  424.4 0.3 convolution_dynamic-update-slice_fusion
  424.7 0.6 convolution_subtract_fusion.1
  425.3 11.7 %cholesky.236 = f32[128,128]{1,0:T(8,128)S(1)} custom-call(f32[128,128]{1,0:T(8,128)S(1)} %cholesky.272), custom_call_target="Cholesky" | custom-call | tf_op jit(solution)/shard_map/jit(cholesky)/cholesky | solution.py:15
  437.0 0.1 copy.33
  437.2 9.8 %custom-call.29 = f32[1,128,128]{1,2,0:T(8,128)S(1)} custom-call(f32[1,128,128]{2,1,0:T(8,128)S(1)} %get-tuple-element.6), custom_call_target="InvertDiagBlocksLowerTriangular" | custom-call | tf_op jit(solution)/shard_map/jit(cholesky)/cholesky | solution.py:15
  447.0 0.3 convolution_dynamic-update-slice_fusion.1
  447.3 0.5 convolution_subtract_fusion.2
  447.8 11.7 %cholesky.253 = f32[128,128]{1,0:T(8,128)S(1)} custom-call(f32[128,128]{1,0:T(8,128)S(1)} %convolution_subtract_fusion.2), custom_call_target="Cholesky" | custom-call | tf_op jit(solution)/shard_map/jit(cholesky)/cholesky | solution.py:15
  459.5 0.1 copy.35
  459.6 0.7 compare_reduce_fusion.1
  460.3 0.6 compare_reduce_fusion
  461.0 0.7 compare_reduce_fusion.2
  464.2 1.1 select_bitcast_fusion
  (13 shorter events, 0.2 us)
Async XLA Ops:
  6.5 253.7 %all-reduce.4.cloned.1.call-start = ((), (), s32[]{:S(2)}) async-start(), calls=%async_computation.1 | async-start | bytes 2097152 | tf_op jit(solution)/shard_map/psum | solution.py:48
  182.4 194.4 %all-reduce.6.cloned.1.call-start = ((), (), s32[]{:S(2)}) async-start(), calls=%async_computation.2 | async-start | bytes 2097152 | tf_op jit(solution)/shard_map/psum | solution.py:48
Sparse Core Ops, SparseCore 0:
  182.5 77.7 all-reduce.3
  263.5 113.2 all-reduce.5
